TPU v7x, 32 devices: a whole 2x2x4 slice. The times are simulated.
32 devices in a mesh: gx: 4 (over z), gy: 8 (over y, x, core).
Axes of the slice: x: 2, y: 2, z: 4, core: 2. Of those that a mesh axis runs over, the one named last changes fastest.
Arguments:
- right_side: float32 [2048, 4096], P('gx', 'gy'), may hold values from -8 to 8
- drift_x: float32 [2048, 4096], P('gx', 'gy'), may hold values from -0.9 to 0.9
- drift_y: float32 [2048, 4096], P('gx', 'gy'), may hold values from -0.9 to 0.9
- sketch_rows: float32 [256, 2048], P(None, 'gx'), may hold values from -0.375 to 0.375
- sketch_cols: float32 [256, 4096], P(None, 'gy'), may hold values from -6 to 6
Outputs:
- solution: float32 [2048, 4096], P('gx', 'gy')
- residual: float32 [2048, 4096], P('gx', 'gy')
All inputs are finite; a program needn't handle non-finite values.
Results may differ from a plain program's by a relative error of at most 0.0003.
Values sent between devices are 32-bit elements; how exact they have to be, the bound alone decides.
A program may use at most 64 MiB of HBM per device.

v0:
```python
import jax
import jax.numpy as jnp
from jax import lax
from jax.sharding import PartitionSpec as P

ITERS = 4


shift_value = 0.05


def padded_2(cells, sides, width):
    for axis, dim in sides:
        count = lax.axis_size(axis)
        ends = count - 1
        head = lax.slice_in_dim(cells, 0, width, axis=dim)
        tail = lax.slice_in_dim(cells, cells.shape[dim] - width, cells.shape[dim], axis=dim)
        cells = jnp.concatenate(
            [
                lax.ppermute(tail, axis, [(i, (i + 1) % count) for i in range(ends)]),
                cells,
                lax.ppermute(head, axis, [((i + 1) % count, i) for i in range(ends)]),
            ],
            axis=dim,
        )
    return cells


def stencil(padded, field, drift_x, drift_y):
    upper_cells = padded[:-2, 1:-1]
    lower_cells = padded[2:, 1:-1]
    left_cells = padded[1:-1, :-2]
    right_cells = padded[1:-1, 2:]
    return (
        (4.0 + shift_value) * field
        - (1.0 + drift_x) * upper_cells
        - (1.0 - drift_x) * lower_cells
        - (1.0 + drift_y) * left_cells
        - (1.0 - drift_y) * right_cells
    )


def solve_small(hessenberg, beta_norm):
    gram_matrix = jnp.dot(hessenberg.T, hessenberg, precision=lax.Precision.HIGHEST)
    target = beta_norm * hessenberg[0]
    factor = jnp.linalg.cholesky(gram_matrix)
    count = hessenberg.shape[1]
    forward = []
    for row in range(count):
        acc = target[row]
        for col in range(row):
            acc = acc - factor[row, col] * forward[col]
        forward.append(acc / factor[row, row])
    backward = [None] * count
    for row in reversed(range(count)):
        acc = forward[row]
        for col in range(row + 1, count):
            acc = acc - factor[col, row] * backward[col]
        backward[row] = acc / factor[row, row]
    return backward


def body(right_side, drift_x, drift_y, sketch_rows, sketch_cols):

    def sketch(field):
        product = jnp.dot(field, sketch_cols.T, precision=lax.Precision.HIGHEST)
        partial_value = jnp.einsum(
            "ki,ik->k", sketch_rows, product, precision=lax.Precision.HIGHEST
        )
        return lax.psum(partial_value, ("gx", "gy"))

    first_sketch = sketch(right_side)
    beta_norm = jnp.sqrt(jnp.sum(first_sketch * first_sketch))
    basis_vectors = [right_side / beta_norm]
    sketched = [first_sketch / beta_norm]
    images = []
    columns = []
    for column in range(ITERS):
        current = basis_vectors[column]
        padded = padded_2(current, (("gx", 0), ("gy", 1)), 1)
        applied = stencil(padded, current, drift_x, drift_y)
        images.append(applied)
        sketch_image = sketch(applied)
        sketch_matrix = jnp.stack(sketched, axis=1)
        projection = jnp.dot(sketch_matrix.T, sketch_image, precision=lax.Precision.HIGHEST)
        remainder = applied
        for index_prev in range(column + 1):
            remainder = remainder - projection[index_prev] * basis_vectors[index_prev]
        remainder_sketch = sketch_image - jnp.dot(
            sketch_matrix, projection, precision=lax.Precision.HIGHEST
        )
        new_norm = jnp.sqrt(jnp.sum(remainder_sketch * remainder_sketch))
        basis_vectors.append(remainder / new_norm)
        sketched.append(remainder_sketch / new_norm)
        entries = jnp.concatenate(
            [projection, new_norm[None], jnp.zeros((ITERS - column - 1,), jnp.float32)]
        )
        columns.append(entries)
    hessenberg = jnp.stack(columns, axis=1)
    coeffs = solve_small(hessenberg, beta_norm)
    solution = jnp.zeros_like(right_side)
    for column in range(ITERS):
        solution = solution + coeffs[column] * basis_vectors[column]
    padded = padded_2(solution, (("gx", 0), ("gy", 1)), 1)
    residual = right_side - stencil(padded, solution, drift_x, drift_y)
    return (solution, residual)


def solution(mesh):
    in_specs = (P("gx", "gy"), P("gx", "gy"), P("gx", "gy"), P(None, "gx"), P(None, "gy"))
    out_specs = (P("gx", "gy"), P("gx", "gy"))
    return jax.shard_map(body, mesh=mesh, in_specs=in_specs, out_specs=out_specs, check_vma=False)
```

profile of v0, /device:TPU:0, one launch (start us, length us, event | category | flops | bytes accessed | tf_op | source)
XLA Modules:
  0.0 366.3 jit_solution(15757160799951034432)
XLA Ops:
  1.7 2.3 convolution_bitcast_fusion.4
  4.3 42.0 %psum.35 = f32[256]{0:T(256)S(1)} all-reduce(f32[256]{0:T(256)S(1)} %multiply_reduce_fusion.4), channel_id=1, replica_groups=mesh['gx'=4,'gy'=8] {'gx','gy'}, use_global_device_ids=true, to_apply=%region_0.0 | all-reduce | flops 256 | bytes 2048 | tf_op jit(solution)/shard_map/psum | solution.py:70
  47.8 3.5 collective-permute-start
  52.7 4.2 %collective-permute-done.1 = f32[1,512]{1,0:T(1,128)S(1)} collective-permute-done((f32[1,512]{1,0:T(1,128)S(1)}, f32[1,512]{1,0:T(1,128)S(1)}, u32[]{:S(2)}, u32[]{:S(2)}) %collective-permute-start.1) | collective-permute-done | bytes 2080 | tf_op jit(solution)/shard_map/ppermute | solution.py:22
  59.6 4.6 %collective-permute-done.3 = f32[514,1]{1,0:T(8,128)S(1)} collective-permute-done((f32[514,1]{1,0:T(8,128)S(1)}, f32[514,1]{1,0:T(8,128)S(1)}, u32[]{:S(2)}, u32[]{:S(2)}) %collective-permute-start.3) | collective-permute-done | bytes 2088 | tf_op jit(solution)/shard_map/ppermute | solution.py:22
  67.4 44.2 %psum.36 = f32[256]{0:T(256)S(1)} all-reduce(f32[256]{0:T(256)S(1)} %multiply_reduce_fusion.3), channel_id=1, replica_groups=mesh['gx'=4,'gy'=8] {'gx','gy'}, use_global_device_ids=true, to_apply=%region_2.0 | all-reduce | flops 256 | bytes 2048 | tf_op jit(solution)/shard_map/psum | solution.py:70
  114.2 2.2 subtract_divide_fusion.2
  116.5 2.7 collective-permute-start.4
  121.1 3.5 collective-permute-done.5
  128.1 3.9 %collective-permute-done.7 = f32[514,1]{1,0:T(8,128)S(1)} collective-permute-done((f32[514,1]{1,0:T(8,128)S(1)}, f32[514,1]{1,0:T(8,128)S(1)}, u32[]{:S(2)}, u32[]{:S(2)}) %collective-permute-start.7) | collective-permute-done | bytes 2088 | tf_op jit(solution)/shard_map/ppermute | solution.py:22
  133.8 1.8 convolution_bitcast_fusion.2
  135.6 2.0 copy.25
  138.8 43.5 %psum.37 = f32[256]{0:T(256)S(1)} all-reduce(f32[256]{0:T(256)S(1)} %multiply_reduce_fusion.2), channel_id=1, replica_groups=mesh['gx'=4,'gy'=8] {'gx','gy'}, use_global_device_ids=true, to_apply=%region_4.0 | all-reduce | flops 256 | bytes 2048 | tf_op jit(solution)/shard_map/psum | solution.py:70
  184.6 2.9 subtract_divide_fusion.1
  187.5 3.4 collective-permute-start.8
  192.2 4.2 %collective-permute-done.9 = f32[1,512]{1,0:T(1,128)S(1)} collective-permute-done((f32[1,512]{1,0:T(1,128)S(1)}, f32[1,512]{1,0:T(1,128)S(1)}, u32[]{:S(2)}, u32[]{:S(2)}) %collective-permute-start.9) | collective-permute-done | bytes 2080 | tf_op jit(solution)/shard_map/ppermute | solution.py:22
  199.4 4.4 %collective-permute-done.11 = f32[514,1]{1,0:T(8,128)S(1)} collective-permute-done((f32[514,1]{1,0:T(8,128)S(1)}, f32[514,1]{1,0:T(8,128)S(1)}, u32[]{:S(2)}, u32[]{:S(2)}) %collective-permute-start.11) | collective-permute-done | bytes 2088 | tf_op jit(solution)/shard_map/ppermute | solution.py:22
  205.6 1.8 convolution_bitcast_fusion.1
  207.4 2.0 copy.30
  210.6 43.6 %psum.38 = f32[256]{0:T(256)S(1)} all-reduce(f32[256]{0:T(256)S(1)} %multiply_reduce_fusion.1), channel_id=1, replica_groups=mesh['gx'=4,'gy'=8] {'gx','gy'}, use_global_device_ids=true, to_apply=%region_6.0 | all-reduce | flops 256 | bytes 2048 | tf_op jit(solution)/shard_map/psum | solution.py:70
  256.4 3.9 %subtract_divide_fusion = f32[512,512]{1,0:T(8,128)S(1)} fusion(f32[512,512]{1,0:T(8,128)} %copy-done.2, f32[512,512]{1,0:T(8,128)S(1)} %subtract_divide_fusion.2, f32[512,512]{1,0:T(8,128)} %copy-done.16, f32[]{:T(128)} %sqrt.18, f32[]{:T(128)} %bitcast.31, f32[]{:T(128)} %bitcast.30, f32[]{:T(128)} %bitcast.29, f32[512,512]{1,0:T(8,128)S(1)} %copy-done.1, ...), kind=kLoop, calls=%fused_computation.92 | loop fusion | flops 2097152 | bytes 5242900 | tf_op jit(solution)/shard_map/div | solution.py:93
  260.3 3.3 collective-permute-start.12
  265.0 4.2 %collective-permute-done.13 = f32[1,512]{1,0:T(1,128)S(1)} collective-permute-done((f32[1,512]{1,0:T(1,128)S(1)}, f32[1,512]{1,0:T(1,128)S(1)}, u32[]{:S(2)}, u32[]{:S(2)}) %collective-permute-start.13) | collective-permute-done | bytes 2080 | tf_op jit(solution)/shard_map/ppermute | solution.py:22
  271.9 4.6 %collective-permute-done.15 = f32[514,1]{1,0:T(8,128)S(1)} collective-permute-done((f32[514,1]{1,0:T(8,128)S(1)}, f32[514,1]{1,0:T(8,128)S(1)}, u32[]{:S(2)}, u32[]{:S(2)}) %collective-permute-start.15) | collective-permute-done | bytes 2088 | tf_op jit(solution)/shard_map/ppermute | solution.py:22
  276.5 2.5 convolution_bitcast_fusion
  279.0 2.0 copy.35
  282.2 43.7 %psum.39 = f32[256]{0:T(256)S(1)} all-reduce(f32[256]{0:T(256)S(1)} %multiply_reduce_fusion), channel_id=1, replica_groups=mesh['gx'=4,'gy'=8] {'gx','gy'}, use_global_device_ids=true, to_apply=%region_8.0 | all-reduce | flops 256 | bytes 2048 | tf_op jit(solution)/shard_map/psum | solution.py:70
  346.2 2.1 multiply_add_fusion
  348.3 3.2 collective-permute-start.16
  352.9 4.2 %collective-permute-done.17 = f32[1,512]{1,0:T(1,128)S(1)} collective-permute-done((f32[1,512]{1,0:T(1,128)S(1)}, f32[1,512]{1,0:T(1,128)S(1)}, u32[]{:S(2)}, u32[]{:S(2)}) %collective-permute-start.17) | collective-permute-done | bytes 2080 | tf_op jit(solution)/shard_map/ppermute | solution.py:22
  359.8 4.6 %collective-permute-done.19 = f32[514,1]{1,0:T(8,128)S(1)} collective-permute-done((f32[514,1]{1,0:T(8,128)S(1)}, f32[514,1]{1,0:T(8,128)S(1)}, u32[]{:S(2)}, u32[]{:S(2)}) %collective-permute-start.19) | collective-permute-done | bytes 2088 | tf_op jit(solution)/shard_map/ppermute | solution.py:22
  364.4 1.9 fusion.2
  (119 shorter events, 43.7 us)
Async XLA Ops:
  4.0 43.6 %copy-start.1 = (f32[512,512]{1,0:T(8,128)S(1)}, f32[512,512]{1,0:T(8,128)}, u32[]{:S(2)}) copy-start(f32[512,512]{1,0:T(8,128)} %param.5) | copy-start | bytes 3145732
  47.6 16.6 %copy-start.8 = (f32[512,512]{1,0:T(8,128)S(1)}, f32[512,512]{1,0:T(8,128)}, u32[]{:S(2)}) copy-start(f32[512,512]{1,0:T(8,128)} %param.6) | copy-start | bytes 3145732
  47.8 16.4 %copy-start.3 = (f32[512,512]{1,0:T(8,128)S(1)}, f32[512,512]{1,0:T(8,128)}, u32[]{:S(2)}) copy-start(f32[512,512]{1,0:T(8,128)} %param.7) | copy-start | bytes 3145732
  47.8 4.8 %collective-permute-start = (f32[1,512]{1,0:T(1,128)S(1)}, f32[1,512]{1,0:T(1,128)S(1)}, u32[]{:S(2)}, u32[]{:S(2)}) collective-permute-start(f32[1,512]{1,0:T(1,128)S(1)} %get-tuple-element.26), channel_id=1, source_target_pairs={{0,8},{8,16},{16,24},{1,9},{9,17},{17,25},{2,10},{10,18},{18,26},{... | collective-permute-start | bytes 6152 | tf_op jit(solution)/shard_map/ppermute | solution.py:20
  51.3 5.5 %collective-permute-start.1 = (f32[1,512]{1,0:T(1,128)S(1)}, f32[1,512]{1,0:T(1,128)S(1)}, u32[]{:S(2)}, u32[]{:S(2)}) collective-permute-start(f32[1,512]{1,0:T(1,128)S(1)} %get-tuple-element.27), channel_id=1, source_target_pairs={{8,0},{16,8},{24,16},{9,1},{17,9},{25,17},{10,2},{18,10},{26,18},{... | collective-permute-start | bytes 6152 | tf_op jit(solution)/shard_map/ppermute | solution.py:22
  57.0 2.6 collective-permute-start.2
  58.3 5.9 %collective-permute-start.3 = (f32[514,1]{1,0:T(8,128)S(1)}, f32[514,1]{1,0:T(8,128)S(1)}, u32[]{:S(2)}, u32[]{:S(2)}) collective-permute-start(f32[514,1]{1,0:T(8,128)S(1)} %get-tuple-element.17), channel_id=1, source_target_pairs={{1,0},{2,1},{3,2},{4,3},{5,4},{6,5},{7,6},{9,8},{10,9},{11,10},{12... | collective-permute-start | bytes 6176 | tf_op jit(solution)/shard_map/ppermute | solution.py:22
  114.2 17.8 %copy-start.9 = (f32[512,512]{1,0:T(8,128)S(1)}, f32[512,512]{1,0:T(8,128)}, u32[]{:S(2)}) copy-start(f32[512,512]{1,0:T(8,128)} %param.6) | copy-start | bytes 3145732
  116.5 4.6 %collective-permute-start.4 = (f32[1,512]{1,0:T(1,128)S(1)}, f32[1,512]{1,0:T(1,128)S(1)}, u32[]{:S(2)}, u32[]{:S(2)}) collective-permute-start(f32[1,512]{1,0:T(1,128)S(1)} %get-tuple-element.24), channel_id=1, source_target_pairs={{0,8},{8,16},{16,24},{1,9},{9,17},{17,25},{2,10},{10,18},{18,26},{... | collective-permute-start | bytes 6152 | tf_op jit(solution)/shard_map/ppermute | solution.py:20
  119.1 5.5 %collective-permute-start.5 = (f32[1,512]{1,0:T(1,128)S(1)}, f32[1,512]{1,0:T(1,128)S(1)}, u32[]{:S(2)}, u32[]{:S(2)}) collective-permute-start(f32[1,512]{1,0:T(1,128)S(1)} %get-tuple-element.25), channel_id=1, source_target_pairs={{8,0},{16,8},{24,16},{9,1},{17,9},{25,17},{10,2},{18,10},{26,18},{... | collective-permute-start | bytes 6152 | tf_op jit(solution)/shard_map/ppermute | solution.py:22
  124.7 3.4 collective-permute-start.6
  126.1 5.9 %collective-permute-start.7 = (f32[514,1]{1,0:T(8,128)S(1)}, f32[514,1]{1,0:T(8,128)S(1)}, u32[]{:S(2)}, u32[]{:S(2)}) collective-permute-start(f32[514,1]{1,0:T(8,128)S(1)} %get-tuple-element.15), channel_id=1, source_target_pairs={{1,0},{2,1},{3,2},{4,3},{5,4},{6,5},{7,6},{9,8},{10,9},{11,10},{12... | collective-permute-start | bytes 6176 | tf_op jit(solution)/shard_map/ppermute | solution.py:22
  184.5 19.2 %copy-start.10 = (f32[512,512]{1,0:T(8,128)S(1)}, f32[512,512]{1,0:T(8,128)}, u32[]{:S(2)}) copy-start(f32[512,512]{1,0:T(8,128)} %param.6) | copy-start | bytes 3145732
  187.5 17.1 %copy-start.2 = (f32[512,512]{1,0:T(8,128)}, f32[512,512]{1,0:T(8,128)S(1)}, u32[]{:S(2)}) copy-start(f32[512,512]{1,0:T(8,128)S(1)} %subtract_divide_fusion.1) | copy-start | bytes 3145732
  187.5 16.3 %copy-start.5 = (f32[512,512]{1,0:T(8,128)S(1)}, f32[512,512]{1,0:T(8,128)}, u32[]{:S(2)}) copy-start(f32[512,512]{1,0:T(8,128)} %param.7) | copy-start | bytes 3145732
  187.5 4.7 %collective-permute-start.8 = (f32[1,512]{1,0:T(1,128)S(1)}, f32[1,512]{1,0:T(1,128)S(1)}, u32[]{:S(2)}, u32[]{:S(2)}) collective-permute-start(f32[1,512]{1,0:T(1,128)S(1)} %get-tuple-element.22), channel_id=1, source_target_pairs={{0,8},{8,16},{16,24},{1,9},{9,17},{17,25},{2,10},{10,18},{18,26},{... | collective-permute-start | bytes 6152 | tf_op jit(solution)/shard_map/ppermute | solution.py:20
  190.9 5.5 %collective-permute-start.9 = (f32[1,512]{1,0:T(1,128)S(1)}, f32[1,512]{1,0:T(1,128)S(1)}, u32[]{:S(2)}, u32[]{:S(2)}) collective-permute-start(f32[1,512]{1,0:T(1,128)S(1)} %get-tuple-element.23), channel_id=1, source_target_pairs={{8,0},{16,8},{24,16},{9,1},{17,9},{25,17},{10,2},{18,10},{26,18},{... | collective-permute-start | bytes 6152 | tf_op jit(solution)/shard_map/ppermute | solution.py:22
  196.5 2.9 collective-permute-start.10
  197.8 5.9 %collective-permute-start.11 = (f32[514,1]{1,0:T(8,128)S(1)}, f32[514,1]{1,0:T(8,128)S(1)}, u32[]{:S(2)}, u32[]{:S(2)}) collective-permute-start(f32[514,1]{1,0:T(8,128)S(1)} %get-tuple-element.13), channel_id=1, source_target_pairs={{1,0},{2,1},{3,2},{4,3},{5,4},{6,5},{7,6},{9,8},{10,9},{11,10},{12... | collective-permute-start | bytes 6176 | tf_op jit(solution)/shard_map/ppermute | solution.py:22
  256.4 20.1 %copy-start.11 = (f32[512,512]{1,0:T(8,128)S(1)}, f32[512,512]{1,0:T(8,128)}, u32[]{:S(2)}) copy-start(f32[512,512]{1,0:T(8,128)} %param.6) | copy-start | bytes 3145732
  260.3 16.2 %copy-start.14 = (f32[512,512]{1,0:T(8,128)}, f32[512,512]{1,0:T(8,128)S(1)}, u32[]{:S(2)}) copy-start(f32[512,512]{1,0:T(8,128)S(1)} %subtract_divide_fusion) | copy-start | bytes 3145732
  260.3 16.2 %copy-start.6 = (f32[512,512]{1,0:T(8,128)S(1)}, f32[512,512]{1,0:T(8,128)}, u32[]{:S(2)}) copy-start(f32[512,512]{1,0:T(8,128)} %param.7) | copy-start | bytes 3145732
  260.3 4.6 %collective-permute-start.12 = (f32[1,512]{1,0:T(1,128)S(1)}, f32[1,512]{1,0:T(1,128)S(1)}, u32[]{:S(2)}, u32[]{:S(2)}) collective-permute-start(f32[1,512]{1,0:T(1,128)S(1)} %get-tuple-element.20), channel_id=1, source_target_pairs={{0,8},{8,16},{16,24},{1,9},{9,17},{17,25},{2,10},{10,18},{18,26},{... | collective-permute-start | bytes 6152 | tf_op jit(solution)/shard_map/ppermute | solution.py:20
  263.6 5.5 %collective-permute-start.13 = (f32[1,512]{1,0:T(1,128)S(1)}, f32[1,512]{1,0:T(1,128)S(1)}, u32[]{:S(2)}, u32[]{:S(2)}) collective-permute-start(f32[1,512]{1,0:T(1,128)S(1)} %get-tuple-element.21), channel_id=1, source_target_pairs={{8,0},{16,8},{24,16},{9,1},{17,9},{25,17},{10,2},{18,10},{26,18},{... | collective-permute-start | bytes 6152 | tf_op jit(solution)/shard_map/ppermute | solution.py:22
  269.3 2.7 collective-permute-start.14
  270.6 5.9 %collective-permute-start.15 = (f32[514,1]{1,0:T(8,128)S(1)}, f32[514,1]{1,0:T(8,128)S(1)}, u32[]{:S(2)}, u32[]{:S(2)}) collective-permute-start(f32[514,1]{1,0:T(8,128)S(1)} %get-tuple-element.11), channel_id=1, source_target_pairs={{1,0},{2,1},{3,2},{4,3},{5,4},{6,5},{7,6},{9,8},{10,9},{11,10},{12... | collective-permute-start | bytes 6176 | tf_op jit(solution)/shard_map/ppermute | solution.py:22
  346.2 18.3 %copy-start.12 = (f32[512,512]{1,0:T(8,128)S(1)}, f32[512,512]{1,0:T(8,128)}, u32[]{:S(2)}) copy-start(f32[512,512]{1,0:T(8,128)} %param.6) | copy-start | bytes 3145732
  348.3 18.0 %copy-start.15 = (f32[512,512]{1,0:T(8,128)}, f32[512,512]{1,0:T(8,128)S(1)}, u32[]{:S(2)}) copy-start(f32[512,512]{1,0:T(8,128)S(1)} %multiply_add_fusion) | copy-start | bytes 3145732
  348.3 4.5 %collective-permute-start.16 = (f32[1,512]{1,0:T(1,128)S(1)}, f32[1,512]{1,0:T(1,128)S(1)}, u32[]{:S(2)}, u32[]{:S(2)}) collective-permute-start(f32[1,512]{1,0:T(1,128)S(1)} %get-tuple-element.18), channel_id=1, source_target_pairs={{0,8},{8,16},{16,24},{1,9},{9,17},{17,25},{2,10},{10,18},{18,26},{... | collective-permute-start | bytes 6152 | tf_op jit(solution)/shard_map/ppermute | solution.py:20
  351.6 5.5 %collective-permute-start.17 = (f32[1,512]{1,0:T(1,128)S(1)}, f32[1,512]{1,0:T(1,128)S(1)}, u32[]{:S(2)}, u32[]{:S(2)}) collective-permute-start(f32[1,512]{1,0:T(1,128)S(1)} %get-tuple-element.19), channel_id=1, source_target_pairs={{8,0},{16,8},{24,16},{9,1},{17,9},{25,17},{10,2},{18,10},{26,18},{... | collective-permute-start | bytes 6152 | tf_op jit(solution)/shard_map/ppermute | solution.py:22
  357.2 2.6 collective-permute-start.18
  358.5 5.9 %collective-permute-start.19 = (f32[514,1]{1,0:T(8,128)S(1)}, f32[514,1]{1,0:T(8,128)S(1)}, u32[]{:S(2)}, u32[]{:S(2)}) collective-permute-start(f32[514,1]{1,0:T(8,128)S(1)} %get-tuple-element.9), channel_id=1, source_target_pairs={{1,0},{2,1},{3,2},{4,3},{5,4},{6,5},{7,6},{9,8},{10,9},{11,10},{12... | collective-permute-start | bytes 6176 | tf_op jit(solution)/shard_map/ppermute | solution.py:22
  (7 other events, 38.2 us)
where the time goes:
time: 372 us; the launch traced here: 366 us
  blocking collectives  217 us (58%)
  waiting for transfers between devices  42.2 us (11%)
  starting transfers between devices  35.7 us (10%)
  other arithmetic  28.1 us (8%)
  between operations  19.8 us (5%)
  local copies, waits for them, and re-layouts  13.1 us (4%)
  matrix products  10.4 us (3%)
    psum x5, blocking collectives, sketch(): return lax.psum(partial_value, ('gx', 'gy'))  217 us
    ppermute x10, waiting for transfers between devices, padded_2(): lax.ppermute(head, axis, [((i + 1) % count, i) for i in range(ends)])  42.2 us
    ppermute x10, starting transfers between devices, padded_2(): lax.ppermute(tail, axis, [(i, (i + 1) % count) for i in range(ends)])  22.6 us
    ppermute x10, starting transfers between devices, padded_2(): lax.ppermute(head, axis, [((i + 1) % count, i) for i in range(ends)])  13.1 us
    unnamed x43, local copies, waits for them, and re-layouts  10.5 us
    dot_general x5, matrix products, sketch(): product = jnp.dot(field, sketch_cols.T, precision=lax.Precision.HIGHEST)  9.45 us
    div x3, other arithmetic, body(): basis_vectors.append(remainder / new_norm)  9.05 us
  transfers between devices with their start and end apart: 20, of which 10 were waited for; matrix products, arithmetic and copies ran while one was open for 0% of the time, Pallas kernels for 0%

commit v1 on v0

v1 whole, which is shorter than its diff:
```python
import jax
import jax.numpy as jnp
from jax import lax
from jax.experimental import pallas as pl
from jax.experimental.pallas import tpu as pltpu
from jax.sharding import PartitionSpec as P

ITERS = 4
CENTER = 4.0 + 0.05
L = 128
PAD = 16
EDGE = 8
MESH = pl.DeviceIdType.MESH
SIDES = [(-1, 0), (1, 0), (0, -1), (0, 1), (-1, -1), (-1, 1), (1, -1), (1, 1)]


def solve_small(gram):
    n = ITERS

    def g(a, b):
        return gram[(min(a, b), max(a, b))]

    f = {}
    for a in range(n + 1):
        for j in range(n):
            value = CENTER * g(a, j) + 2.0 * g(a, j + 1)
            f[a, j] = value + 2.0 * g(a, j - 1) if j else value
    m = {}
    for i in range(n):
        for j in range(i + 1):
            value = CENTER * f[i, j] + 2.0 * f[i + 1, j]
            m[i, j] = value + 2.0 * f[i - 1, j] if i else value
    inv, low, scaled = [], {}, {}
    for j in range(n):
        for i in range(j, n):
            acc = m[i, j]
            for k in range(j):
                acc = acc - scaled[i, k] * low[j, k]
            scaled[i, j] = acc
        inv.append(1.0 / scaled[j, j])
        for i in range(j + 1, n):
            low[i, j] = scaled[i, j] * inv[j]
    forward = []
    for i in range(n):
        acc = f[0, i]
        for k in range(i):
            acc = acc - low[i, k] * forward[k]
        forward.append(acc)
    y = [None] * n
    for i in reversed(range(n)):
        acc = forward[i] * inv[i]
        for k in range(i + 1, n):
            acc = acc - low[k, i] * y[k]
        y[i] = acc
    res = []
    for k in range(n + 1):
        z = 0.0
        if k < n:
            z = z + CENTER * y[k]
        if k >= 1:
            z = z + 2.0 * y[k - 1]
        if k + 1 < n:
            z = z + 2.0 * y[k + 1]
        res.append(1.0 - z if k == 0 else -z)
    return y, res


def kernel(nx, ny, b_hbm, dx_hbm, dy_hbm, rows_hbm, cols_hbm, x_hbm, r_hbm,
           ext, basis, rows_v, cols_v, rows_t, ct_hi, ct_lo, col_out, col_in, diag_out, diag_in,
           part, got_x, sum_x, got_y, x_v, r_v,
           in_sem, out_sem, hs_sem, hr_sem, xs_sem, xr_sem, ys_sem, yr_sem):
    gx, gy = lax.axis_index("gx"), lax.axis_index("gy")
    height, width = b_hbm.shape
    groups = width // L
    sketch_dim = rows_hbm.shape[0]
    last = groups
    block = 128
    blocks = height // block

    loads = []
    for a, src in enumerate((b_hbm, dx_hbm, dy_hbm)):
        for p in range(groups):
            copy = pltpu.make_async_copy(
                src.at[:, pl.ds(p * L, L)], ext.at[a, p, pl.ds(PAD, height), :], in_sem.at[a * groups + p])
            copy.start()
            loads.append(copy)
    for s, (src, dst) in enumerate(((cols_hbm, cols_v), (rows_hbm, rows_v))):
        copy = pltpu.make_async_copy(src, dst, in_sem.at[3 * groups + s])
        copy.start()
        loads.append(copy)

    def device(ox, oy):
        return {"gx": lax.rem(gx + (ox + nx), nx), "gy": lax.rem(gy + (oy + ny), ny)}

    peers = {(sx % nx, sy % ny) for sx, sy in SIDES}
    peers |= {(o, 0) for o in range(1, nx)} | {(0, o) for o in range(1, ny)}
    barrier = pltpu.get_barrier_semaphore()
    for ox, oy in sorted(peers):
        pl.semaphore_signal(barrier, inc=1, device_id=device(ox, oy), device_id_type=MESH)

    lane = lax.broadcasted_iota(jnp.int32, (EDGE, L), 1)
    tall_lane = lax.broadcasted_iota(jnp.int32, (height, L), 1)
    one, zero = jnp.float32(1.0), jnp.float32(0.0)
    has_up = jnp.where(gx > 0, one, zero)
    has_down = jnp.where(gx < nx - 1, one, zero)
    has_left = jnp.where(gy > 0, one, zero)
    has_right = jnp.where(gy < ny - 1, one, zero)
    col_mask = jnp.where(lane < L // 2, has_right, has_left)
    empty = jnp.zeros((EDGE, L), jnp.float32)
    bottom = PAD + height
    for p in range(groups + 1):
        for at in (0, bottom + EDGE):
            ext[0, p, pl.ds(at, EDGE), :] = empty
            for k in range(ITERS - 1):
                basis[k, p, pl.ds(at, EDGE), :] = empty
    part[...] = jnp.zeros_like(part)

    for copy in loads[: 3 * groups]:
        copy.wait()
    for a in range(3):
        packed = jnp.where(
            tall_lane < L // 2, ext[a, 0, pl.ds(PAD, height), :], ext[a, groups - 1, pl.ds(PAD, height), :])
        diag_out[0, a] = packed[:EDGE]
        diag_out[1, a] = packed[height - EDGE:]
        turned = jnp.transpose(packed)
        col_out[0, a] = turned[:EDGE]
        col_out[1, a] = turned[L - EDGE:]
    pl.semaphore_wait(barrier, len(peers))

    sends = []
    for d, (sx, sy) in enumerate(SIDES):
        if sy == 0:
            src_at, dst_at = (PAD, bottom) if sx < 0 else (bottom - EDGE, PAD - EDGE)
            src = ext.at[:, pl.ds(0, groups), pl.ds(src_at, EDGE), :]
            dst = ext.at[:, pl.ds(0, groups), pl.ds(dst_at, EDGE), :]
        elif sx == 0:
            src, dst = col_out.at[int(sy > 0)], col_in.at[int(sy > 0)]
        else:
            src, dst = diag_out.at[int(sx > 0)], diag_in.at[d - 4]
        copy = pltpu.make_async_remote_copy(
            src_ref=src, dst_ref=dst, send_sem=hs_sem.at[d], recv_sem=hr_sem.at[d],
            device_id=device(sx, sy), device_id_type=MESH)
        copy.start()
        sends.append(copy)

    for copy in loads[3 * groups:]:
        copy.wait()
    turned_cols = jnp.transpose(cols_v[...])
    high = turned_cols.astype(jnp.bfloat16)
    ct_hi[...] = high
    ct_lo[...] = (turned_cols - high.astype(jnp.float32)).astype(jnp.bfloat16)
    rows_t[...] = jnp.transpose(rows_v[...])

    def sketch_block(view, i):
        field = jnp.concatenate(
            [view[p, pl.ds(PAD + i * block, block), :] for p in range(groups)], axis=1)
        hi = field.astype(jnp.bfloat16)
        lo = (field - hi.astype(jnp.float32)).astype(jnp.bfloat16)
        dot = lambda u, v: jnp.dot(u, v, preferred_element_type=jnp.float32)
        product = dot(hi, ct_hi[...]) + dot(hi, ct_lo[...]) + dot(lo, ct_hi[...])
        product = product * rows_t[pl.ds(i * block, block), :]
        return jnp.sum(product.reshape(block // 8, 8, sketch_dim), axis=0)

    def view_of(k):
        return ext.at[0] if k == 0 else basis.at[k - 1]

    def stencil(k, at, row_mask=None):
        src, out = view_of(k - 1), view_of(k)
        mid = [src[p, pl.ds(at, EDGE), :] for p in range(groups + 1)]
        from_left = [pltpu.roll(v, 1, 1) for v in mid]
        from_right = [pltpu.roll(v, L - 1, 1) for v in mid]
        for p in range(groups + 1 if k < ITERS else groups):
            left = jnp.where(lane == 0, from_left[p - 1], from_left[p])
            right = jnp.where(lane == L - 1, from_right[(p + 1) % (groups + 1)], from_right[p])
            up = src[p, pl.ds(at - 1, EDGE), :]
            down = src[p, pl.ds(at + 1, EDGE), :]
            total = (up + down) + ext[1, p, pl.ds(at, EDGE), :] * (up - down)
            total = total + ((left + right) + ext[2, p, pl.ds(at, EDGE), :] * (left - right))
            value = -0.5 * total
            if k >= 2:
                value = value - view_of(k - 2)[p, pl.ds(at, EDGE), :]
            if p == last:
                value = value * col_mask
            if row_mask is not None:
                value = value * row_mask
            out[p, pl.ds(at, EDGE), :] = value

    def close(k, total):
        part[pl.ds(k, 1), :] = jnp.sum(total, axis=0, keepdims=True)

    nothing = jnp.zeros((8, sketch_dim), jnp.float32)
    close(0, lax.fori_loop(0, blocks, lambda i, t: t + sketch_block(view_of(0), i), nothing))

    for copy in sends:
        copy.wait()
    gap = jnp.zeros((L - 2 * EDGE, height), jnp.float32)
    for a in range(3):
        beside = jnp.transpose(jnp.concatenate([col_in[0, a], gap, col_in[1, a]], axis=0))
        if a == 0:
            beside = beside * jnp.where(tall_lane < L // 2, has_right, has_left)
        ext[a, last, pl.ds(PAD, height), :] = beside
        above = jnp.where(lane < L // 2, diag_in[2, a], diag_in[3, a])
        below = jnp.where(lane < L // 2, diag_in[0, a], diag_in[1, a])
        if a == 0:
            above, below = above * col_mask, below * col_mask
        ext[a, last, pl.ds(PAD - EDGE, EDGE), :] = above
        ext[a, last, pl.ds(bottom, EDGE), :] = below
    for p in range(groups + 1):
        ext[0, p, pl.ds(PAD - EDGE, EDGE), :] = ext[0, p, pl.ds(PAD - EDGE, EDGE), :] * has_up
        ext[0, p, pl.ds(bottom, EDGE), :] = ext[0, p, pl.ds(bottom, EDGE), :] * has_down

    for k in range(1, ITERS + 1):
        if k < ITERS:
            stencil(k, PAD - EDGE, has_up)
            stencil(k, bottom, has_down)

        def step(i, total, k=k):
            for s in range(block // EDGE):
                stencil(k, PAD + i * block + s * EDGE)
            return total + sketch_block(view_of(k - 1), i) if k >= 2 else total

        total = lax.fori_loop(0, blocks, step, nothing)
        if k >= 2:
            close(k - 1, total)
    close(ITERS, lax.fori_loop(0, blocks, lambda i, t: t + sketch_block(view_of(ITERS), i), nothing))

    def exchange(src, got, send, recv, count, along):
        copies = []
        for o in range(1, count):
            copy = pltpu.make_async_remote_copy(
                src_ref=src, dst_ref=got.at[o - 1], send_sem=send.at[o - 1], recv_sem=recv.at[o - 1],
                device_id=device(*((o, 0) if along == 0 else (0, o))), device_id_type=MESH)
            copy.start()
            copies.append(copy)
        for copy in copies:
            copy.wait()
        total = src[...]
        for o in range(1, count):
            total = total + got[o - 1]
        return total

    sum_x[...] = exchange(part, got_x, xs_sem, xr_sem, nx, 0)
    whole = exchange(sum_x, got_y, ys_sem, yr_sem, ny, 1)

    gram = {}
    for a in range(ITERS + 1):
        for c in range(a, ITERS + 1):
            entry = jnp.sum(whole[a:a + 1] * whole[c:c + 1], axis=1, keepdims=True)
            gram[a, c] = jnp.broadcast_to(entry, (EDGE, L))
    y, res = solve_small(gram)

    def combine(i, _):
        for p in range(groups):
            for s in range(4):
                at = i * 32 + s * EDGE
                v = [view_of(k)[p, pl.ds(PAD + at, EDGE), :] for k in range(ITERS + 1)]
                x, r = y[0] * v[0], res[0] * v[0]
                for k in range(1, ITERS + 1):
                    if k < ITERS:
                        x = x + y[k] * v[k]
                    r = r + res[k] * v[k]
                x_v[p, pl.ds(at, EDGE), :] = x
                r_v[p, pl.ds(at, EDGE), :] = r
        return 0

    stores = []
    for q in range(blocks):
        lax.fori_loop(q * (block // 32), (q + 1) * (block // 32), combine, 0)
        for o, (src, dst) in enumerate(((x_v, x_hbm), (r_v, r_hbm))):
            for p in range(groups):
                copy = pltpu.make_async_copy(
                    src.at[p, pl.ds(q * block, block), :],
                    dst.at[pl.ds(q * block, block), pl.ds(p * L, L)],
                    out_sem.at[(q * 2 + o) * groups + p])
                copy.start()
                stores.append(copy)
    for copy in stores:
        copy.wait()


def solution(mesh):
    nx, ny = mesh.shape["gx"], mesh.shape["gy"]

    def body(right_side, drift_x, drift_y, sketch_rows, sketch_cols):
        height, width = right_side.shape
        groups = width // L
        dim = sketch_rows.shape[0]
        tall = height + 2 * PAD
        f32, bf16 = jnp.float32, jnp.bfloat16
        dma = pltpu.SemaphoreType.DMA
        out = jax.ShapeDtypeStruct((height, width), f32)
        return pl.pallas_call(
            lambda *refs: kernel(nx, ny, *refs),
            out_shape=(out, out),
            in_specs=[pl.BlockSpec(memory_space=pl.ANY)] * 5,
            out_specs=[pl.BlockSpec(memory_space=pl.ANY)] * 2,
            scratch_shapes=[
                pltpu.VMEM((3, groups + 1, tall, L), f32),
                pltpu.VMEM((ITERS, groups + 1, tall, L), f32),
                pltpu.VMEM((dim, height), f32),
                pltpu.VMEM((dim, width), f32),
                pltpu.VMEM((height, dim), f32),
                pltpu.VMEM((width, dim), bf16),
                pltpu.VMEM((width, dim), bf16),
                pltpu.VMEM((2, 3, EDGE, height), f32),
                pltpu.VMEM((2, 3, EDGE, height), f32),
                pltpu.VMEM((2, 3, EDGE, L), f32),
                pltpu.VMEM((4, 3, EDGE, L), f32),
                pltpu.VMEM((8, dim), f32),
                pltpu.VMEM((nx - 1, 8, dim), f32),
                pltpu.VMEM((8, dim), f32),
                pltpu.VMEM((ny - 1, 8, dim), f32),
                pltpu.VMEM((groups, height, L), f32),
                pltpu.VMEM((groups, height, L), f32),
                dma((3 * groups + 2,)),
                dma((2 * groups * (height // 128),)),
                dma((8,)), dma((8,)),
                dma((nx - 1,)), dma((nx - 1,)),
                dma((ny - 1,)), dma((ny - 1,)),
            ],
            compiler_params=pltpu.CompilerParams(
                collective_id=0, has_side_effects=True, vmem_limit_bytes=48 * 1024 * 1024),
        )(right_side, drift_x, drift_y, sketch_rows, sketch_cols)

    in_specs = (P("gx", "gy"), P("gx", "gy"), P("gx", "gy"), P(None, "gx"), P(None, "gy"))
    out_specs = (P("gx", "gy"), P("gx", "gy"))
    return jax.shard_map(body, mesh=mesh, in_specs=in_specs, out_specs=out_specs, check_vma=False)
```

time: 372 us -> 34.9 us (0.09); the launches traced: 366 us -> 34.6 us
  blocking collectives: 217 us -> 0 us
  waiting for transfers between devices: 42.2 us -> 0 us
  starting transfers between devices: 35.7 us -> 0 us
  other arithmetic: 28.1 us -> 0 us
  Pallas kernels: 0 us -> 27.5 us
  between operations: 19.8 us -> 0.65 us
  matrix products: 10.4 us -> 0 us
  local copies, waits for them, and re-layouts: 13.1 us -> 6.47 us
    psum x5 -> x0, blocking collectives: 217 us -> none  [sketch(): return lax.psum(partial_value, ('gx', 'gy'))]
    ppermute x20 -> x0, waiting for transfers between devices: 42.2 us -> none  [the longest x10 42.2 us: padded_2(): lax.ppermute(head, axis, [((i + 1) % count, i) for i in range(ends)])]
    ppermute x20 -> x0, starting transfers between devices: 35.7 us -> none  [the longest x10 22.6 us: padded_2(): lax.ppermute(tail, axis, [(i, (i + 1) % count) for i in range(ends)])]
    pallas_call x0 -> x1, Pallas kernels: none -> 27.5 us  [body(): pl.pallas_call(lambda *refs: kernel(nx, ny, *refs), out_shape=(out, out),...]
    dot_general x12 -> x0, matrix products: 10.4 us -> none  [the longest x5 9.45 us: sketch(): product = jnp.dot(field, sketch_cols.T, precision=lax.Precision.HIGHEST)]
    div x8 -> x0, other arithmetic: 9.82 us -> none  [the longest x3 9.05 us: body(): basis_vectors.append(remainder / new_norm)]
    sub x4 -> x0, other arithmetic: 4.45 us -> none  [the longest x3 2.55 us: stencil(): (4.0 + shift_value) * field - (1.0 + drift_x) * upper_cells]
    dot_general x6 -> x0, other arithmetic: 4.37 us -> none  [the longest x5 3.77 us: sketch(): jnp.einsum('ki,ik->k', sketch_rows, product, precision=lax.Precision.HIGH...]
  transfers between devices with their start and end apart: 20 -> 0, of which waited for: 10 -> 0; matrix products, arithmetic and copies ran while one was open for 0% -> 0% of each run, Pallas kernels for 0% -> 0%
where the time goes in v1:
time: 34.9 us; the launch traced here: 34.6 us
  Pallas kernels  27.5 us (79%)
  local copies, waits for them, and re-layouts  6.47 us (19%)
  between operations  0.65 us (2%)
    pallas_call x1, Pallas kernels, body(): pl.pallas_call(lambda *refs: kernel(nx, ny, *refs), out_shape=(out, out),...  27.5 us
    unnamed x10, local copies, waits for them, and re-layouts  6.47 us

profile of v1, /device:TPU:0, one launch (start us, length us, event | category | flops | bytes accessed | tf_op | source)
XLA Modules:
  0.0 34.6 jit_solution(13146651835247640734)
XLA Ops:
  0.6 0.0 copy-start
  0.6 1.2 %copy-done = f32[512,512]{1,0:T(8,128)S(1)} copy-done((f32[512,512]{1,0:T(8,128)S(1)}, f32[512,512]{1,0:T(8,128)}, u32[]{:S(2)}) %copy-start) | copy-done | bytes 1048600
  1.9 0.0 copy-start.1
  1.9 1.2 %copy-done.1 = f32[512,512]{1,0:T(8,128)S(1)} copy-done((f32[512,512]{1,0:T(8,128)S(1)}, f32[512,512]{1,0:T(8,128)}, u32[]{:S(2)}) %copy-start.1) | copy-done | bytes 1048600
  3.1 0.0 copy-start.2
  3.1 1.0 %copy-done.2 = f32[256,512]{1,0:T(8,128)S(1)} copy-done((f32[256,512]{1,0:T(8,128)S(1)}, f32[256,512]{1,0:T(8,128)}, u32[]{:S(2)}) %copy-start.2) | copy-done | bytes 524312
  4.1 0.0 copy-start.3
  4.1 1.0 %copy-done.3 = f32[256,512]{1,0:T(8,128)S(1)} copy-done((f32[256,512]{1,0:T(8,128)S(1)}, f32[256,512]{1,0:T(8,128)}, u32[]{:S(2)}) %copy-start.3) | copy-done | bytes 524312
  5.2 27.5 %shard_map.68 = (f32[512,512]{1,0:T(8,128)S(1)}, f32[512,512]{1,0:T(8,128)S(1)}) custom-call(f32[512,512]{1,0:T(8,128)S(1)} %copy-done, f32[512,512]{1,0:T(8,128)S(1)} %copy-done.1, f32[512,512]{1,0:T(8,128)} %refs_2_.1, f32[256,512]{1,0:T(8,128)S(1)} %copy-done.2, f32[256,512]{1,0:T(8,128)S(1)} %copy-done.3), custom_call_target="tpu_custom_call" | custom-call | tf_op jit(solution)/shard_map/pallas_call | solution.py:292
  32.7 1.0 %copy.9 = f32[512,512]{1,0:T(8,128)} copy(f32[512,512]{1,0:T(8,128)S(1)} %get-tuple-element.4) | data formatting | bytes 2097152
  33.6 1.0 %copy.10 = f32[512,512]{1,0:T(8,128)} copy(f32[512,512]{1,0:T(8,128)S(1)} %get-tuple-element.5) | data formatting | bytes 2097152
Async XLA Ops:
  0.6 1.2 %copy-start = (f32[512,512]{1,0:T(8,128)S(1)}, f32[512,512]{1,0:T(8,128)}, u32[]{:S(2)}) copy-start(f32[512,512]{1,0:T(8,128)} %refs_0_.1) | copy-start | bytes 3145732
  1.9 1.2 %copy-start.1 = (f32[512,512]{1,0:T(8,128)S(1)}, f32[512,512]{1,0:T(8,128)}, u32[]{:S(2)}) copy-start(f32[512,512]{1,0:T(8,128)} %refs_1_.1) | copy-start | bytes 3145732
  3.1 1.0 %copy-start.2 = (f32[256,512]{1,0:T(8,128)S(1)}, f32[256,512]{1,0:T(8,128)}, u32[]{:S(2)}) copy-start(f32[256,512]{1,0:T(8,128)} %refs_3_.1) | copy-start | bytes 1572868
  4.1 1.0 %copy-start.3 = (f32[256,512]{1,0:T(8,128)S(1)}, f32[256,512]{1,0:T(8,128)}, u32[]{:S(2)}) copy-start(f32[256,512]{1,0:T(8,128)} %refs_4_.1) | copy-start | bytes 1572868

commit v2 on v1

--- a/solution.py
+++ b/solution.py
@@ -65,10 +65,9 @@
     return y, res
 
 
-def kernel(nx, ny, b_hbm, dx_hbm, dy_hbm, rows_hbm, cols_hbm, x_hbm, r_hbm,
-           ext, basis, rows_v, cols_v, rows_t, ct_hi, ct_lo, col_out, col_in, diag_out, diag_in,
-           part, got_x, sum_x, got_y, x_v, r_v,
-           in_sem, out_sem, hs_sem, hr_sem, xs_sem, xr_sem, ys_sem, yr_sem):
+def kernel(nx, ny, b_hbm, dx_hbm, dy_hbm, rows_hbm, cols_hbm, basis_all, coefs,
+           ext, rows_v, cols_v, rows_t, ct_hi, ct_lo, col_out, col_in, diag_out, diag_in,
+           part, got_x, sum_x, got_y, in_sem, hs_sem, hr_sem, xs_sem, xr_sem, ys_sem, yr_sem):
     gx, gy = lax.axis_index("gx"), lax.axis_index("gy")
     height, width = b_hbm.shape
     groups = width // L
@@ -76,6 +75,7 @@
     last = groups
     block = 128
     blocks = height // block
+    basis = basis_all.at[pl.ds(1, ITERS)]
 
     loads = []
     for a, src in enumerate((b_hbm, dx_hbm, dy_hbm)):
@@ -117,6 +117,10 @@
 
     for copy in loads[: 3 * groups]:
         copy.wait()
+    keep = pltpu.make_async_copy(
+        ext.at[0, pl.ds(0, groups), pl.ds(PAD, height), :],
+        basis_all.at[0, pl.ds(0, groups), pl.ds(PAD, height), :], in_sem.at[3 * groups + 2])
+    keep.start()
     for a in range(3):
         packed = jnp.where(
             tall_lane < L // 2, ext[a, 0, pl.ds(PAD, height), :], ext[a, groups - 1, pl.ds(PAD, height), :])
@@ -248,12 +252,22 @@
             entry = jnp.sum(whole[a:a + 1] * whole[c:c + 1], axis=1, keepdims=True)
             gram[a, c] = jnp.broadcast_to(entry, (EDGE, L))
     y, res = solve_small(gram)
-
-    def combine(i, _):
+    for k, value in enumerate(y + res):
+        coefs[k] = value
+    keep.wait()
+
+
+def combine(basis, coefs, x_hbm, r_hbm, x_v, r_v, sem):
+    groups, height = x_v.shape[0], x_v.shape[1]
+    block = 128
+
+    def rows(i, _):
+        y = [coefs[k] for k in range(ITERS)]
+        res = [coefs[ITERS + k] for k in range(ITERS + 1)]
         for p in range(groups):
             for s in range(4):
                 at = i * 32 + s * EDGE
-                v = [view_of(k)[p, pl.ds(PAD + at, EDGE), :] for k in range(ITERS + 1)]
+                v = [basis[k, p, pl.ds(PAD + at, EDGE), :] for k in range(ITERS + 1)]
                 x, r = y[0] * v[0], res[0] * v[0]
                 for k in range(1, ITERS + 1):
                     if k < ITERS:
@@ -264,14 +278,14 @@
         return 0
 
     stores = []
-    for q in range(blocks):
-        lax.fori_loop(q * (block // 32), (q + 1) * (block // 32), combine, 0)
+    for q in range(height // block):
+        lax.fori_loop(q * (block // 32), (q + 1) * (block // 32), rows, 0)
         for o, (src, dst) in enumerate(((x_v, x_hbm), (r_v, r_hbm))):
             for p in range(groups):
                 copy = pltpu.make_async_copy(
                     src.at[p, pl.ds(q * block, block), :],
                     dst.at[pl.ds(q * block, block), pl.ds(p * L, L)],
-                    out_sem.at[(q * 2 + o) * groups + p])
+                    sem.at[(q * 2 + o) * groups + p])
                 copy.start()
                 stores.append(copy)
     for copy in stores:
@@ -288,15 +302,18 @@
         tall = height + 2 * PAD
         f32, bf16 = jnp.float32, jnp.bfloat16
         dma = pltpu.SemaphoreType.DMA
-        out = jax.ShapeDtypeStruct((height, width), f32)
-        return pl.pallas_call(
+        pieces = height // 128
+        hbm = pltpu.HBM((height, width), f32)
+        args = [pltpu.with_memory_space_constraint(v, pltpu.HBM)
+                for v in (right_side, drift_x, drift_y, sketch_rows, sketch_cols)]
+        basis, coefs = pl.pallas_call(
             lambda *refs: kernel(nx, ny, *refs),
-            out_shape=(out, out),
-            in_specs=[pl.BlockSpec(memory_space=pl.ANY)] * 5,
-            out_specs=[pl.BlockSpec(memory_space=pl.ANY)] * 2,
+            out_shape=(
+                pltpu.VMEM((ITERS + 1, groups + 1, tall, L), f32), pltpu.VMEM((2 * ITERS + 1, EDGE, L), f32)),
+            in_specs=[pl.BlockSpec(memory_space=pltpu.HBM)] * 5,
+            out_specs=[pl.BlockSpec(memory_space=pltpu.VMEM)] * 2,
             scratch_shapes=[
                 pltpu.VMEM((3, groups + 1, tall, L), f32),
-                pltpu.VMEM((ITERS, groups + 1, tall, L), f32),
                 pltpu.VMEM((dim, height), f32),
                 pltpu.VMEM((dim, width), f32),
                 pltpu.VMEM((height, dim), f32),
@@ -310,17 +327,24 @@
                 pltpu.VMEM((nx - 1, 8, dim), f32),
                 pltpu.VMEM((8, dim), f32),
                 pltpu.VMEM((ny - 1, 8, dim), f32),
-                pltpu.VMEM((groups, height, L), f32),
-                pltpu.VMEM((groups, height, L), f32),
-                dma((3 * groups + 2,)),
-                dma((2 * groups * (height // 128),)),
+                dma((3 * groups + 3,)),
                 dma((8,)), dma((8,)),
                 dma((nx - 1,)), dma((nx - 1,)),
                 dma((ny - 1,)), dma((ny - 1,)),
             ],
             compiler_params=pltpu.CompilerParams(
-                collective_id=0, has_side_effects=True, vmem_limit_bytes=48 * 1024 * 1024),
-        )(right_side, drift_x, drift_y, sketch_rows, sketch_cols)
+                collective_id=0, has_side_effects=True, vmem_limit_bytes=40 * 1024 * 1024),
+        )(*args)
+        return pl.pallas_call(
+            combine,
+            out_shape=(hbm, hbm),
+            in_specs=[pl.BlockSpec(memory_space=pltpu.VMEM)] * 2,
+            out_specs=[pl.BlockSpec(memory_space=pltpu.HBM)] * 2,
+            scratch_shapes=[
+                pltpu.VMEM((groups, height, L), f32), pltpu.VMEM((groups, height, L), f32),
+                dma((2 * groups * pieces,))],
+            compiler_params=pltpu.CompilerParams(vmem_limit_bytes=8 * 1024 * 1024),
+        )(basis, coefs)
 
     in_specs = (P("gx", "gy"), P("gx", "gy"), P("gx", "gy"), P(None, "gx"), P(None, "gy"))
     out_specs = (P("gx", "gy"), P("gx", "gy"))

time: 34.9 us -> 28.4 us (0.81)
  local copies, waits for them, and re-layouts: 6.47 us -> 0 us
    unnamed x10 -> x0, local copies, waits for them, and re-layouts: 6.47 us -> none
    pallas_call x1 -> x2, Pallas kernels: 27.5 us -> 27.6 us  [the longest x1 25.9 us: body(): pl.pallas_call(lambda *refs: kernel(nx, ny, *refs), out_shape=(pltpu.VMEM...]
where the time goes in v2:
time: 28.4 us; the launch traced here: 28.3 us
  Pallas kernels  27.6 us (97%)
  between operations  0.64 us (2%)
    pallas_call x1, Pallas kernels, body(): pl.pallas_call(lambda *refs: kernel(nx, ny, *refs), out_shape=(pltpu.VMEM...  25.9 us
    pallas_call x1, Pallas kernels, body(): pl.pallas_call(combine, out_shape=(hbm, hbm), in_specs=[pl.BlockSpec(memo...  1.73 us

profile of v2, /device:TPU:0, one launch (start us, length us, event | category | flops | bytes accessed | tf_op | source)
XLA Modules:
  0.0 28.3 jit_solution(6986706982263770757)
XLA Ops:
  0.6 25.9 %shard_map.68 = (f32[5,5,544,128]{3,2,1,0:T(8,128)S(1)}, f32[9,8,128]{2,1,0:T(8,128)S(1)}) custom-call(f32[512,512]{1,0:T(8,128)} %refs_0_.1, f32[512,512]{1,0:T(8,128)} %refs_1_.1, f32[512,512]{1,0:T(8,128)} %refs_2_.1, f32[256,512]{1,0:T(8,128)} %refs_3_.1, f32[256,512]{1,0:T(8,128)} %refs_4_.1), custom_call_target="tpu_custom_call" | custom-call | tf_op jit(solution)/shard_map/pallas_call | solution.py:309
  26.5 1.7 %shard_map.69 = (f32[512,512]{1,0:T(8,128)}, f32[512,512]{1,0:T(8,128)}) custom-call(f32[5,5,544,128]{3,2,1,0:T(8,128)S(1)} %get-tuple-element.4.basis, f32[9,8,128]{2,1,0:T(8,128)S(1)} %get-tuple-element.5.coefs), custom_call_target="tpu_custom_call" | custom-call | tf_op jit(solution)/shard_map/pallas_call | solution.py:338

commit v3 on v2

--- a/solution.py
+++ b/solution.py
@@ -11,6 +11,7 @@
 PAD = 16
 EDGE = 8
 MESH = pl.DeviceIdType.MESH
+PIECES = [pl.ds(0, ITERS - 1), pl.ds(8, 2)]
 SIDES = [(-1, 0), (1, 0), (0, -1), (0, 1), (-1, -1), (-1, 1), (1, -1), (1, 1)]
 
 
@@ -78,8 +79,9 @@
     basis = basis_all.at[pl.ds(1, ITERS)]
 
     loads = []
-    for a, src in enumerate((b_hbm, dx_hbm, dy_hbm)):
-        for p in range(groups):
+    order = [0, groups - 1] + list(range(1, groups - 1))
+    for p in order:
+        for a, src in enumerate((b_hbm, dx_hbm, dy_hbm)):
             copy = pltpu.make_async_copy(
                 src.at[:, pl.ds(p * L, L)], ext.at[a, p, pl.ds(PAD, height), :], in_sem.at[a * groups + p])
             copy.start()
@@ -95,9 +97,6 @@
     peers = {(sx % nx, sy % ny) for sx, sy in SIDES}
     peers |= {(o, 0) for o in range(1, nx)} | {(0, o) for o in range(1, ny)}
     barrier = pltpu.get_barrier_semaphore()
-    for ox, oy in sorted(peers):
-        pl.semaphore_signal(barrier, inc=1, device_id=device(ox, oy), device_id_type=MESH)
-
     lane = lax.broadcasted_iota(jnp.int32, (EDGE, L), 1)
     tall_lane = lax.broadcasted_iota(jnp.int32, (height, L), 1)
     one, zero = jnp.float32(1.0), jnp.float32(0.0)
@@ -108,6 +107,15 @@
     col_mask = jnp.where(lane < L // 2, has_right, has_left)
     empty = jnp.zeros((EDGE, L), jnp.float32)
     bottom = PAD + height
+    diag_in[...] = jnp.zeros_like(diag_in)
+    col_in[...] = jnp.zeros_like(col_in)
+    for p in range(groups):
+        for a in range(3):
+            ext[a, p, pl.ds(PAD - EDGE, EDGE), :] = empty
+            ext[a, p, pl.ds(bottom, EDGE), :] = empty
+    for ox, oy in sorted(peers):
+        pl.semaphore_signal(barrier, inc=1, device_id=device(ox, oy), device_id_type=MESH)
+
     for p in range(groups + 1):
         for at in (0, bottom + EDGE):
             ext[0, p, pl.ds(at, EDGE), :] = empty
@@ -115,12 +123,8 @@
                 basis[k, p, pl.ds(at, EDGE), :] = empty
     part[...] = jnp.zeros_like(part)
 
-    for copy in loads[: 3 * groups]:
+    for copy in loads[:6]:
         copy.wait()
-    keep = pltpu.make_async_copy(
-        ext.at[0, pl.ds(0, groups), pl.ds(PAD, height), :],
-        basis_all.at[0, pl.ds(0, groups), pl.ds(PAD, height), :], in_sem.at[3 * groups + 2])
-    keep.start()
     for a in range(3):
         packed = jnp.where(
             tall_lane < L // 2, ext[a, 0, pl.ds(PAD, height), :], ext[a, groups - 1, pl.ds(PAD, height), :])
@@ -131,8 +135,11 @@
         col_out[1, a] = turned[L - EDGE:]
     pl.semaphore_wait(barrier, len(peers))
 
+    def inside(sx, sy):
+        return (gx + sx >= 0) & (gx + sx < nx) & (gy + sy >= 0) & (gy + sy < ny)
+
     sends = []
-    for d, (sx, sy) in enumerate(SIDES):
+    for d, (sx, sy) in reversed(list(enumerate(SIDES))):
         if sy == 0:
             src_at, dst_at = (PAD, bottom) if sx < 0 else (bottom - EDGE, PAD - EDGE)
             src = ext.at[:, pl.ds(0, groups), pl.ds(src_at, EDGE), :]
@@ -144,8 +151,15 @@
         copy = pltpu.make_async_remote_copy(
             src_ref=src, dst_ref=dst, send_sem=hs_sem.at[d], recv_sem=hr_sem.at[d],
             device_id=device(sx, sy), device_id_type=MESH)
-        copy.start()
-        sends.append(copy)
+        if d == 1:
+            for load in loads[6:3 * groups]:
+                load.wait()
+        pl.when(inside(sx, sy))(copy.start)
+        sends.append((copy, sx, sy))
+    keep = pltpu.make_async_copy(
+        ext.at[0, pl.ds(0, groups), pl.ds(PAD, height), :],
+        basis_all.at[0, pl.ds(0, groups), pl.ds(PAD, height), :], in_sem.at[3 * groups + 2])
+    keep.start()
 
     for copy in loads[3 * groups:]:
         copy.wait()
@@ -190,34 +204,58 @@
             out[p, pl.ds(at, EDGE), :] = value
 
     def close(k, total):
-        part[pl.ds(k, 1), :] = jnp.sum(total, axis=0, keepdims=True)
+        part[pl.ds(k if k < ITERS - 1 else 8 + k - (ITERS - 1), 1), :] = jnp.sum(total, axis=0, keepdims=True)
 
     nothing = jnp.zeros((8, sketch_dim), jnp.float32)
     close(0, lax.fori_loop(0, blocks, lambda i, t: t + sketch_block(view_of(0), i), nothing))
 
-    for copy in sends:
-        copy.wait()
+    for copy, sx, sy in sends:
+        pl.when(inside(-sx, -sy))(copy.wait_recv)
+    for copy, sx, sy in sends:
+        pl.when(inside(sx, sy))(copy.wait_send)
     gap = jnp.zeros((L - 2 * EDGE, height), jnp.float32)
     for a in range(3):
         beside = jnp.transpose(jnp.concatenate([col_in[0, a], gap, col_in[1, a]], axis=0))
-        if a == 0:
-            beside = beside * jnp.where(tall_lane < L // 2, has_right, has_left)
         ext[a, last, pl.ds(PAD, height), :] = beside
         above = jnp.where(lane < L // 2, diag_in[2, a], diag_in[3, a])
         below = jnp.where(lane < L // 2, diag_in[0, a], diag_in[1, a])
-        if a == 0:
-            above, below = above * col_mask, below * col_mask
         ext[a, last, pl.ds(PAD - EDGE, EDGE), :] = above
         ext[a, last, pl.ds(bottom, EDGE), :] = below
-    for p in range(groups + 1):
-        ext[0, p, pl.ds(PAD - EDGE, EDGE), :] = ext[0, p, pl.ds(PAD - EDGE, EDGE), :] * has_up
-        ext[0, p, pl.ds(bottom, EDGE), :] = ext[0, p, pl.ds(bottom, EDGE), :] * has_down
+    def start(src, got, send, recv, count, along, piece):
+        copies = []
+        rows = PIECES[piece]
+        for o in range(1, count):
+            copy = pltpu.make_async_remote_copy(
+                src_ref=src.at[rows], dst_ref=got.at[o - 1, rows],
+                send_sem=send.at[piece, o - 1], recv_sem=recv.at[piece, o - 1],
+                device_id=device(*((o, 0) if along == 0 else (0, o))), device_id_type=MESH)
+            copy.start()
+            copies.append(copy)
+        return copies
+
+    def finish(copies, src, got, piece):
+        rows = PIECES[piece]
+        for copy in copies:
+            copy.wait()
+        total = src[rows]
+        for o in range(len(copies)):
+            total = total + got[o, rows]
+        return total
+
+    def along_x(piece):
+        return start(part, got_x, xs_sem, xr_sem, nx, 0, piece)
+
+    def along_y(piece):
+        return start(sum_x, got_y, ys_sem, yr_sem, ny, 1, piece)
 
     for k in range(1, ITERS + 1):
         if k < ITERS:
             stencil(k, PAD - EDGE, has_up)
             stencil(k, bottom, has_down)
 
+        if k == ITERS:
+            early = along_x(0)
+
         def step(i, total, k=k):
             for s in range(block // EDGE):
                 stencil(k, PAD + i * block + s * EDGE)
@@ -228,28 +266,18 @@
             close(k - 1, total)
     close(ITERS, lax.fori_loop(0, blocks, lambda i, t: t + sketch_block(view_of(ITERS), i), nothing))
 
-    def exchange(src, got, send, recv, count, along):
-        copies = []
-        for o in range(1, count):
-            copy = pltpu.make_async_remote_copy(
-                src_ref=src, dst_ref=got.at[o - 1], send_sem=send.at[o - 1], recv_sem=recv.at[o - 1],
-                device_id=device(*((o, 0) if along == 0 else (0, o))), device_id_type=MESH)
-            copy.start()
-            copies.append(copy)
-        for copy in copies:
-            copy.wait()
-        total = src[...]
-        for o in range(1, count):
-            total = total + got[o - 1]
-        return total
-
-    sum_x[...] = exchange(part, got_x, xs_sem, xr_sem, nx, 0)
-    whole = exchange(sum_x, got_y, ys_sem, yr_sem, ny, 1)
+    late = along_x(1)
+    sum_x[PIECES[0]] = finish(early, part, got_x, 0)
+    early = along_y(0)
+    sum_x[PIECES[1]] = finish(late, part, got_x, 1)
+    late = along_y(1)
+    sums = finish(early, sum_x, got_y, 0), finish(late, sum_x, got_y, 1)
+    whole = [piece[k:k + 1] for piece in sums for k in range(piece.shape[0])]
 
     gram = {}
     for a in range(ITERS + 1):
         for c in range(a, ITERS + 1):
-            entry = jnp.sum(whole[a:a + 1] * whole[c:c + 1], axis=1, keepdims=True)
+            entry = jnp.sum(whole[a] * whole[c], axis=1, keepdims=True)
             gram[a, c] = jnp.broadcast_to(entry, (EDGE, L))
     y, res = solve_small(gram)
     for k, value in enumerate(y + res):
@@ -323,14 +351,14 @@
                 pltpu.VMEM((2, 3, EDGE, height), f32),
                 pltpu.VMEM((2, 3, EDGE, L), f32),
                 pltpu.VMEM((4, 3, EDGE, L), f32),
-                pltpu.VMEM((8, dim), f32),
-                pltpu.VMEM((nx - 1, 8, dim), f32),
-                pltpu.VMEM((8, dim), f32),
-                pltpu.VMEM((ny - 1, 8, dim), f32),
+                pltpu.VMEM((16, dim), f32),
+                pltpu.VMEM((nx - 1, 16, dim), f32),
+                pltpu.VMEM((16, dim), f32),
+                pltpu.VMEM((ny - 1, 16, dim), f32),
                 dma((3 * groups + 3,)),
                 dma((8,)), dma((8,)),
-                dma((nx - 1,)), dma((nx - 1,)),
-                dma((ny - 1,)), dma((ny - 1,)),
+                dma((2, nx - 1)), dma((2, nx - 1)),
+                dma((2, ny - 1)), dma((2, ny - 1)),
             ],
             compiler_params=pltpu.CompilerParams(
                 collective_id=0, has_side_effects=True, vmem_limit_bytes=40 * 1024 * 1024),

time: 28.4 us -> 24.6 us (0.87)
  Pallas kernels: 27.6 us -> 23.8 us
    pallas_call x1, Pallas kernels: 25.9 us -> 22.1 us  [body(): pl.pallas_call(lambda *refs: kernel(nx, ny, *refs), out_shape=(pltpu.VMEM...]
where the time goes in v3:
time: 24.6 us; the launch traced here: 24.5 us
  Pallas kernels  23.8 us (97%)
  between operations  0.64 us (3%)
    pallas_call x1, Pallas kernels, body(): pl.pallas_call(lambda *refs: kernel(nx, ny, *refs), out_shape=(pltpu.VMEM...  22.1 us
    pallas_call x1, Pallas kernels, body(): pl.pallas_call(combine, out_shape=(hbm, hbm), in_specs=[pl.BlockSpec(memo...  1.73 us

profile of v3, /device:TPU:0, one launch (start us, length us, event | category | flops | bytes accessed | tf_op | source)
XLA Modules:
  0.0 24.5 jit_solution(17270827002976394180)
XLA Ops:
  0.6 22.1 %shard_map.68 = (f32[5,5,544,128]{3,2,1,0:T(8,128)S(1)}, f32[9,8,128]{2,1,0:T(8,128)S(1)}) custom-call(f32[512,512]{1,0:T(8,128)} %refs_0_.1, f32[512,512]{1,0:T(8,128)} %refs_1_.1, f32[512,512]{1,0:T(8,128)} %refs_2_.1, f32[256,512]{1,0:T(8,128)} %refs_3_.1, f32[256,512]{1,0:T(8,128)} %refs_4_.1), custom_call_target="tpu_custom_call" | custom-call | tf_op jit(solution)/shard_map/pallas_call | solution.py:337
  22.7 1.7 %shard_map.69 = (f32[512,512]{1,0:T(8,128)}, f32[512,512]{1,0:T(8,128)}) custom-call(f32[5,5,544,128]{3,2,1,0:T(8,128)S(1)} %get-tuple-element.4.basis, f32[9,8,128]{2,1,0:T(8,128)S(1)} %get-tuple-element.5.coefs), custom_call_target="tpu_custom_call" | custom-call | tf_op jit(solution)/shard_map/pallas_call | solution.py:366

commit v4 on v3

--- a/solution.py
+++ b/solution.py
@@ -11,7 +11,7 @@
 PAD = 16
 EDGE = 8
 MESH = pl.DeviceIdType.MESH
-PIECES = [pl.ds(0, ITERS - 1), pl.ds(8, 2)]
+PIECES = [pl.ds(0, ITERS), pl.ds(8, 1)]
 SIDES = [(-1, 0), (1, 0), (0, -1), (0, 1), (-1, -1), (-1, 1), (1, -1), (1, 1)]
 
 
@@ -94,8 +94,11 @@
     def device(ox, oy):
         return {"gx": lax.rem(gx + (ox + nx), nx), "gy": lax.rem(gy + (oy + ny), ny)}
 
-    peers = {(sx % nx, sy % ny) for sx, sy in SIDES}
-    peers |= {(o, 0) for o in range(1, nx)} | {(0, o) for o in range(1, ny)}
+    def inside(sx, sy):
+        return (gx + sx >= 0) & (gx + sx < nx) & (gy + sy >= 0) & (gy + sy < ny)
+
+    peers = [(o, 0) for o in range(1, nx)] + [(0, o) for o in range(1, ny)]
+    corners = SIDES[4:]
     barrier = pltpu.get_barrier_semaphore()
     lane = lax.broadcasted_iota(jnp.int32, (EDGE, L), 1)
     tall_lane = lax.broadcasted_iota(jnp.int32, (height, L), 1)
@@ -113,9 +116,13 @@
         for a in range(3):
             ext[a, p, pl.ds(PAD - EDGE, EDGE), :] = empty
             ext[a, p, pl.ds(bottom, EDGE), :] = empty
-    for ox, oy in sorted(peers):
+    def greet(ox, oy):
         pl.semaphore_signal(barrier, inc=1, device_id=device(ox, oy), device_id_type=MESH)
 
+    for ox, oy in peers:
+        greet(ox, oy)
+    for sx, sy in corners:
+        pl.when(inside(sx, sy))(lambda sx=sx, sy=sy: greet(sx, sy))
     for p in range(groups + 1):
         for at in (0, bottom + EDGE):
             ext[0, p, pl.ds(at, EDGE), :] = empty
@@ -133,10 +140,10 @@
         turned = jnp.transpose(packed)
         col_out[0, a] = turned[:EDGE]
         col_out[1, a] = turned[L - EDGE:]
-    pl.semaphore_wait(barrier, len(peers))
-
-    def inside(sx, sy):
-        return (gx + sx >= 0) & (gx + sx < nx) & (gy + sy >= 0) & (gy + sy < ny)
+    greeted = len(peers)
+    for sx, sy in corners:
+        greeted = greeted + inside(sx, sy).astype(jnp.int32)
+    pl.semaphore_wait(barrier, greeted)
 
     sends = []
     for d, (sx, sy) in reversed(list(enumerate(SIDES))):
@@ -204,7 +211,7 @@
             out[p, pl.ds(at, EDGE), :] = value
 
     def close(k, total):
-        part[pl.ds(k if k < ITERS - 1 else 8 + k - (ITERS - 1), 1), :] = jnp.sum(total, axis=0, keepdims=True)
+        part[pl.ds(k if k < ITERS else 8, 1), :] = jnp.sum(total, axis=0, keepdims=True)
 
     nothing = jnp.zeros((8, sketch_dim), jnp.float32)
     close(0, lax.fori_loop(0, blocks, lambda i, t: t + sketch_block(view_of(0), i), nothing))
@@ -253,18 +260,21 @@
             stencil(k, PAD - EDGE, has_up)
             stencil(k, bottom, has_down)
 
+        def rows(i, k=k):
+            for s in range(block // EDGE):
+                stencil(k, PAD + i * block + s * EDGE)
+
+        def step(i, total, k=k):
+            rows(i)
+            return total + sketch_block(view_of(k), i - 1)
+
+        rows(0)
+        if k >= 2:
+            close(k - 1, total + sketch_block(view_of(k - 1), blocks - 1))
         if k == ITERS:
             early = along_x(0)
-
-        def step(i, total, k=k):
-            for s in range(block // EDGE):
-                stencil(k, PAD + i * block + s * EDGE)
-            return total + sketch_block(view_of(k - 1), i) if k >= 2 else total
-
-        total = lax.fori_loop(0, blocks, step, nothing)
-        if k >= 2:
-            close(k - 1, total)
-    close(ITERS, lax.fori_loop(0, blocks, lambda i, t: t + sketch_block(view_of(ITERS), i), nothing))
+        total = lax.fori_loop(1, blocks, step, nothing)
+    close(ITERS, total + sketch_block(view_of(ITERS), blocks - 1))
 
     late = along_x(1)
     sum_x[PIECES[0]] = finish(early, part, got_x, 0)

time: 24.6 us -> 26.1 us (1.061)
  Pallas kernels: 23.8 us -> 25.3 us
    pallas_call x1, Pallas kernels: 22.1 us -> 23.6 us  [body(): pl.pallas_call(lambda *refs: kernel(nx, ny, *refs), out_shape=(pltpu.VMEM...]
where the time goes in v4:
time: 26.1 us; the launch traced here: 26 us
  Pallas kernels  25.3 us (97%)
  between operations  0.64 us (2%)
    pallas_call x1, Pallas kernels, body(): pl.pallas_call(lambda *refs: kernel(nx, ny, *refs), out_shape=(pltpu.VMEM...  23.6 us
    pallas_call x1, Pallas kernels, body(): pl.pallas_call(combine, out_shape=(hbm, hbm), in_specs=[pl.BlockSpec(memo...  1.73 us

profile of v4, /device:TPU:0, one launch (start us, length us, event | category | flops | bytes accessed | tf_op | source)
XLA Modules:
  0.0 26.0 jit_solution(18235348996841369053)
XLA Ops:
  0.6 23.6 %shard_map.68 = (f32[5,5,544,128]{3,2,1,0:T(8,128)S(1)}, f32[9,8,128]{2,1,0:T(8,128)S(1)}) custom-call(f32[512,512]{1,0:T(8,128)} %refs_0_.1, f32[512,512]{1,0:T(8,128)} %refs_1_.1, f32[512,512]{1,0:T(8,128)} %refs_2_.1, f32[256,512]{1,0:T(8,128)} %refs_3_.1, f32[256,512]{1,0:T(8,128)} %refs_4_.1), custom_call_target="tpu_custom_call" | custom-call | tf_op jit(solution)/shard_map/pallas_call | solution.py:347
  24.2 1.7 %shard_map.69 = (f32[512,512]{1,0:T(8,128)}, f32[512,512]{1,0:T(8,128)}) custom-call(f32[5,5,544,128]{3,2,1,0:T(8,128)S(1)} %get-tuple-element.4.basis, f32[9,8,128]{2,1,0:T(8,128)S(1)} %get-tuple-element.5.coefs), custom_call_target="tpu_custom_call" | custom-call | tf_op jit(solution)/shard_map/pallas_call | solution.py:376

commit v5 on v4

--- a/solution.py
+++ b/solution.py
@@ -265,12 +265,13 @@
                 stencil(k, PAD + i * block + s * EDGE)
 
         def step(i, total, k=k):
+            total = total + sketch_block(view_of(k), i - 1)
             rows(i)
-            return total + sketch_block(view_of(k), i - 1)
-
-        rows(0)
+            return total
+
         if k >= 2:
             close(k - 1, total + sketch_block(view_of(k - 1), blocks - 1))
+        rows(0)
         if k == ITERS:
             early = along_x(0)
         total = lax.fori_loop(1, blocks, step, nothing)

time: 26.1 us -> 23.6 us (0.904)
  Pallas kernels: 25.3 us -> 22.8 us
    pallas_call x1, Pallas kernels: 23.6 us -> 21.1 us  [body(): pl.pallas_call(lambda *refs: kernel(nx, ny, *refs), out_shape=(pltpu.VMEM...]
where the time goes in v5:
time: 23.6 us; the launch traced here: 23.5 us
  Pallas kernels  22.8 us (97%)
  between operations  0.64 us (3%)
    pallas_call x1, Pallas kernels, body(): pl.pallas_call(lambda *refs: kernel(nx, ny, *refs), out_shape=(pltpu.VMEM...  21.1 us
    pallas_call x1, Pallas kernels, body(): pl.pallas_call(combine, out_shape=(hbm, hbm), in_specs=[pl.BlockSpec(memo...  1.73 us

profile of v5, /device:TPU:0, one launch (start us, length us, event | category | flops | bytes accessed | tf_op | source)
XLA Modules:
  0.0 23.5 jit_solution(13220225082005550259)
XLA Ops:
  0.6 21.1 %shard_map.68 = (f32[5,5,544,128]{3,2,1,0:T(8,128)S(1)}, f32[9,8,128]{2,1,0:T(8,128)S(1)}) custom-call(f32[512,512]{1,0:T(8,128)} %refs_0_.1, f32[512,512]{1,0:T(8,128)} %refs_1_.1, f32[512,512]{1,0:T(8,128)} %refs_2_.1, f32[256,512]{1,0:T(8,128)} %refs_3_.1, f32[256,512]{1,0:T(8,128)} %refs_4_.1), custom_call_target="tpu_custom_call" | custom-call | tf_op jit(solution)/shard_map/pallas_call | solution.py:348
  21.7 1.7 %shard_map.69 = (f32[512,512]{1,0:T(8,128)}, f32[512,512]{1,0:T(8,128)}) custom-call(f32[5,5,544,128]{3,2,1,0:T(8,128)S(1)} %get-tuple-element.4.basis, f32[9,8,128]{2,1,0:T(8,128)S(1)} %get-tuple-element.5.coefs), custom_call_target="tpu_custom_call" | custom-call | tf_op jit(solution)/shard_map/pallas_call | solution.py:377
